TPU v7x, 256 devices: a whole 4x4x8 slice. The times are simulated.
256 devices in a mesh: dp: 8 (over x, core), code: 32 (over z, y).
Axes of the slice: x: 4, y: 4, z: 8, core: 2. Of those that a mesh axis runs over, the one named last changes fastest.
Arguments:
- latents: bfloat16 [4096, 256], P(('dp', 'code')), may hold values from -1000 to 1000
- out_grad: bfloat16 [4096, 256], P(('dp', 'code')), may hold values from -6 to 6
- targets: int32 [4096], P('dp'), may hold values from 0 to 262143
- codebook: bfloat16 [262144, 256], P('code'), may hold values from -2 to 2
Outputs:
- latent_grad: bfloat16 [4096, 256], P(('dp', 'code'))
- codebook_grad: float32 [262144, 256], P(('code', 'dp'))
- token_loss: float32 [4096], P(('dp', 'code'))
All inputs are finite; a program needn't handle non-finite values.
Results may differ from a plain program's by a relative error of at most 0.0042.
Values may be sent and summed in bfloat16 or wider, within the bound.
No kernel may reach another device: no remote copies, remote signals or barrier semaphores. Data moves between devices by JAX's collectives and lax.ppermute only.
A program may use at most 128 MiB of HBM per device.

v0:
```python
import jax
import jax.numpy as jnp
from jax import lax
from jax.sharding import PartitionSpec as P

ce_weight = 1.0


def per_device(latents, out_grad, targets, codebook):
    lat_all, grad_all = (
        lax.all_gather(latents, "code", axis=0, tiled=True),
        lax.all_gather(out_grad, "code", axis=0, tiled=True),
    )
    code_dev, feature_width = codebook.shape
    groups = lax.axis_size("dp")
    blocks = max(1, code_dev // 2048)
    sub_rows = code_dev // groups
    block_rows = sub_rows // blocks
    local_ids = targets - lax.axis_index("code") * code_dev
    layered = codebook.reshape(groups, blocks, block_rows, feature_width)
    dims_nt = (((1,), (1,)), ((), ()))

    def block_parts(block):
        book_block = layered[:, block].reshape(groups * block_rows, feature_width)
        code_ids = (
            jnp.arange(groups, dtype=jnp.int32)[:, None] * sub_rows
            + block * block_rows
            + jnp.arange(block_rows, dtype=jnp.int32)[None, :]
        ).reshape(-1)
        hit_mask = local_ids[:, None] == code_ids[None, :]
        logit_block = lax.dot_general(
            lat_all, book_block, dims_nt, preferred_element_type=jnp.float32
        )
        back_block = lax.dot_general(
            grad_all, book_block, dims_nt, preferred_element_type=jnp.float32
        )
        return (book_block, hit_mask, logit_block, back_block)

    tok_count = lat_all.shape[0]
    top = jnp.full((tok_count,), -jnp.inf, jnp.float32)
    total = jnp.zeros((tok_count,), jnp.float32)
    weighted = jnp.zeros((tok_count,), jnp.float32)
    picked = jnp.zeros((tok_count,), jnp.float32)
    for block in range(blocks):
        book_block, hit_mask, logit_block, back_block = block_parts(block)
        new_top = jnp.maximum(top, jnp.max(logit_block, axis=1))
        factor = jnp.exp(top - new_top)
        expo = jnp.exp(logit_block - new_top[:, None])
        total = total * factor + jnp.sum(expo, axis=1)
        weighted = weighted * factor + jnp.sum(expo * back_block, axis=1)
        picked = picked + jnp.sum(jnp.where(hit_mask, logit_block, 0.0), axis=1)
        top = new_top
    peak_value = lax.pmax(top, "code")
    rescale = jnp.exp(top - peak_value)
    total, weighted, picked = lax.psum((total * rescale, weighted * rescale, picked), "code")
    lse = peak_value + jnp.log(total)
    mean_back = weighted / total
    own_count = latents.shape[0]
    token_loss = lax.dynamic_slice_in_dim(
        lse - picked, lax.axis_index("code") * own_count, own_count, 0
    )
    valid = (local_ids >= 0) & (local_ids < code_dev)
    segment_ids = jnp.where(valid, local_ids, code_dev)
    direct = jax.ops.segment_sum(
        grad_all.astype(jnp.float32), segment_ids, num_segments=code_dev + 1
    )[:code_dev]
    direct = direct.reshape(groups, blocks, block_rows, feature_width)
    lat_grad = jnp.zeros((tok_count, feature_width), jnp.float32)
    collected = []
    for block in range(blocks):
        book_block, hit_mask, logit_block, back_block = block_parts(block)
        probs = jnp.exp(logit_block - lse[:, None])
        delta = probs * (back_block - mean_back[:, None]) + ce_weight * (
            probs - hit_mask.astype(jnp.float32)
        )
        delta = delta.astype(jnp.bfloat16)
        lat_grad = lat_grad + jnp.dot(delta, book_block, preferred_element_type=jnp.float32)
        term = lax.dot_general(
            delta, lat_all, (((0,), (0,)), ((), ())), preferred_element_type=jnp.float32
        )
        term = term + direct[:, block].reshape(groups * block_rows, feature_width)
        collected.append(term.reshape(groups, 1, block_rows, feature_width))
    whole = jnp.concatenate(collected, axis=1).reshape(code_dev, feature_width)
    codebook_grad = lax.psum_scatter(whole, "dp", scatter_dimension=0, tiled=True)
    latent_grad = lax.psum_scatter(lat_grad, "code", scatter_dimension=0, tiled=True).astype(
        jnp.bfloat16
    )
    return (latent_grad, codebook_grad, token_loss)


def solution(mesh):
    in_specs = (P(("dp", "code"), None), P(("dp", "code"), None), P("dp"), P("code", None))
    out_specs = (P(("dp", "code"), None), P(("code", "dp"), None), P(("dp", "code")))
    return jax.shard_map(
        per_device, mesh=mesh, in_specs=in_specs, out_specs=out_specs, check_vma=False
    )
```

profile of v0, /device:TPU:1, one launch (start us, length us, event | category | flops | bytes accessed | tf_op | source)
XLA Modules:
  0.0 585.0 jit_solution(4853329677700653990)
XLA Ops:
  7.3 41.3 %all_gather.6 = bf16[512,256]{1,0:T(8,128)(2,1)S(1)} all-gather(bf16[16,256]{1,0:T(8,128)(2,1)} %param.4), channel_id=1, replica_groups=mesh['dp'=8,'code'=32] {'code'}, dimensions={0}, use_global_device_ids=true | all-gather | bytes 270336 | tf_op jit(solution)/shard_map/all_gather | solution.py:11
  48.6 36.1 %all_gather.7 = bf16[512,256]{1,0:T(8,128)(2,1)S(1)} all-gather(bf16[16,256]{1,0:T(8,128)(2,1)} %param.5), channel_id=1, replica_groups=mesh['dp'=8,'code'=32] {'code'}, dimensions={0}, use_global_device_ids=true | all-gather | bytes 270336 | tf_op jit(solution)/shard_map/all_gather | solution.py:12
  84.7 3.6 fusion.26
  88.2 2.7 fusion.33
  90.9 2.7 fusion.31
  93.6 2.7 fusion.28
  96.3 2.7 fusion.30
  99.0 2.7 fusion.32
  101.7 2.7 fusion.29
  104.8 2.7 fusion.27
  107.5 58.1 %pmax.7 = f32[512]{0:T(512)S(1)} all-reduce(f32[512]{0:T(512)S(1)} %get-tuple-element.22), channel_id=1, replica_groups=mesh['dp'=8,'code'=32] {'code'}, use_global_device_ids=true, to_apply=%region_4.5 | all-reduce | flops 512 | bytes 4096 | tf_op jit(solution)/shard_map/pmax | solution.py:53
  165.6 13.2 %fusion.18 = (f32[512]{0:T(512)S(1)}, f32[512]{0:T(512)S(1)}, f32[512]{0:T(512)S(1)}, f32[512]{0:T(512)S(1)}, f32[512]{0:T(512)S(1)}, /*index=5*/f32[512]{0:T(51...) fusion(f32[512,2048]{1,0:T(8,128)} %get-tuple-element.50, ...), kind=kOutput, calls=%fused_computation.36 | convolution fusion | flops 566224896 | bytes 34932736 | tf_op jit(solution)/shard_map/dot_general | solution.py:34
  178.8 57.1 %all-reduce = (f32[512]{0:T(512)S(1)}, f32[512]{0:T(512)S(1)}, f32[512]{0:T(512)S(1)}) all-reduce(f32[512]{0:T(512)S(1)} %get-tuple-element.34, f32[512]{0:T(512)S(1)} %get-tuple-element.33, f32[512]{0:T(512)S(1)} %add_add_fusion), channel_id=1, replica_groups=mesh['dp'=8,'code'=32] {'code'}, use_global_device_ids=true, to_apply=%region_14.15 | all-reduce | flops 1536 | bytes 12288 | tf_op jit(solution)/shard_map/psum | solution.py:55
  236.0 13.5 %fusion.16 = (bf16[512,2048]{1,0:T(8,128)(2,1)S(1)}, bf16[512,2048]{1,0:T(8,128)(2,1)S(1)}, bf16[512,2048]{1,0:T(8,128)(2,1)S(1)}, bf16[512,2048]{1,0:T(8,128)(2,1)S(1)}) fusion(f32[512,2048]{1,0:T(8,128)} %fusion.33, f32[512,2048]{1,0:T(8,128)} %get-tuple-element.52, s32[2048]{0:T(1024)S(1)} %bitcast.85, f32[512]{0:T(512)S(1)} %get-tuple-element.39, ...), kind=kLoop, calls=%fused_computation.26 | loop fusion | flops 33554432 | bytes 41981952 | tf_op jit(solution)/shard_map/convert_element_type | solution.py:76
  249.5 2.8 fusion.34
  252.4 1.9 convolution_add_fusion.6
  254.4 0.7 convolution_add_fusion.5
  255.1 1.5 convolution_add_fusion.4
  256.7 8.2 %scatter_custom_fusion = f32[8193,256]{1,0:T(8,128)} fusion(s32[512]{0:T(512)S(1)} %get-tuple-element.20, f32[]{:T(128)} %constant.11.clone.1, bf16[512,256]{1,0:T(8,128)(2,1)} %copy-done.9), kind=kCustom, calls=%fused_computation.10 | custom fusion | flops 262144 | bytes 8651780 | tf_op jit(solution)/shard_map/scatter-add | solution.py:64
  264.9 3.4 slice-done
  268.3 2.1 fusion.25
  270.4 2.5 convolution_add_fusion.2
  273.0 0.8 convolution_add_fusion.1
  273.7 0.8 copy-done.1
  274.6 0.7 convolution_add_fusion.3
  275.3 0.8 convolution_add_fusion
  276.1 0.8 pad_maximum_fusion
  276.9 3.8 copy.8
  280.8 0.6 dynamic_slice.3
  281.3 235.7 %reduce-scatter.3.cloned.1.call-done = f32[16,256]{1,0:T(8,128)} async-done(((f32[512,256]{1,0:T(8,128)}), f32[16,256]{1,0:T(8,128)}) %reduce-scatter.3.cloned.1.call-update) | async-done | bytes 16400 | tf_op jit(solution)/shard_map/reduce_scatter | solution.py:85
  517.0 1.3 convert_element_type.38
  518.4 59.8 %reduce-scatter.5.cloned.1.call-done = f32[1024,256]{1,0:T(8,128)} async-done(((f32[8192,256]{1,0:T(8,128)}), f32[1024,256]{1,0:T(8,128)}) %reduce-scatter.5.cloned.1.call-update) | async-done | bytes 1048592 | tf_op jit(solution)/shard_map/reduce_scatter | solution.py:84
  (47 shorter events, 0.5 us)
Async XLA Ops:
  7.2 509.9 %reduce-scatter.3.cloned.1.call-start = ((), (), s32[]{:S(2)}) async-start(), calls=%async_computation.2 | async-start | bytes 540672 | tf_op jit(solution)/shard_map/reduce_scatter | solution.py:85
  84.7 14.3 %copy-start.9 = (bf16[512,256]{1,0:T(8,128)(2,1)}, bf16[512,256]{1,0:T(8,128)(2,1)S(1)}, u32[]{:S(2)}) copy-start(bf16[512,256]{1,0:T(8,128)(2,1)S(1)} %all_gather.7) | copy-start | bytes 786436
  88.2 8.1 %copy-start.8 = (bf16[8,1,256,256]{3,2,1,0:T(8,128)(2,1)}, bf16[8,1,256,256]{3,2,1,0:T(8,128)(2,1)S(1)}, u32[]{:S(2)}) copy-start(bf16[8,1,256,256]{3,2,1,0:T(8,128)(2,1)S(1)} %get-tuple-element.29) | copy-start | bytes 3145732
  88.2 13.5 %copy-start.6 = (bf16[8,1,256,256]{3,2,1,0:T(8,128)(2,1)}, bf16[8,1,256,256]{3,2,1,0:T(8,128)(2,1)S(1)}, u32[]{:S(2)}) copy-start(bf16[8,1,256,256]{3,2,1,0:T(8,128)(2,1)S(1)} %get-tuple-element.31) | copy-start | bytes 3145732
  99.0 5.7 copy-start.11
  104.4 61.2 %copy-start.12 = (s32[512]{0:T(512)S(1)}, s32[512]{0:T(512)}, u32[]{:S(2)}) copy-start(s32[512]{0:T(512)} %param.6) | copy-start | bytes 6148
  104.4 61.2 %copy-start.10 = (bf16[512,256]{1,0:T(8,128)(2,1)S(1)}, bf16[512,256]{1,0:T(8,128)(2,1)}, u32[]{:S(2)}) copy-start(bf16[512,256]{1,0:T(8,128)(2,1)} %copy-done.9) | copy-start | bytes 786436
  249.5 4.8 copy-start
  249.5 4.8 copy-start.4
  249.5 4.8 copy-start.2
  249.5 4.8 copy-start.7
  256.7 321.5 %reduce-scatter.5.cloned.1.call-start = ((), (), s32[]{:S(2)}) async-start(), calls=%async_computation.3 | async-start | bytes 9437184 | tf_op jit(solution)/shard_map/reduce_scatter | solution.py:84
  264.9 3.4 slice-start
  268.3 2.1 copy-start.5
  270.4 2.5 copy-start.3
  273.0 1.6 copy-start.1
Sparse Core Ops, SparseCore 0:
  256.8 260.2 reduce-scatter.2
  520.2 57.9 reduce-scatter.4
where the time goes:
time: 585 us
  waiting for transfers between devices  296 us (51%)
  blocking collectives  193 us (33%)
  matrix products  43.9 us (8%)
  other arithmetic  24.2 us (4%)
  local copies, waits for them, and re-layouts  14.4 us (2%)
  between operations  14.3 us (2%)
    reduce_scatter x1, waiting for transfers between devices, per_device(): lax.psum_scatter(lat_grad, 'code', scatter_dimension=0, tiled=True)  236 us
    reduce_scatter x1, waiting for transfers between devices, per_device(): lax.psum_scatter(whole, 'dp', scatter_dimension=0, tiled=True)  59.8 us
    pmax x1, blocking collectives, per_device(): peak_value = lax.pmax(top, 'code')  58.1 us
    psum x1, blocking collectives, per_device(): lax.psum((total * rescale, weighted * rescale, picked), 'code')  57.1 us
    all_gather x1, blocking collectives, per_device(): lax.all_gather(latents, 'code', axis=0, tiled=True)  41.3 us
    all_gather x1, blocking collectives, per_device(): lax.all_gather(out_grad, 'code', axis=0, tiled=True)  36.1 us
    dot_general x4, matrix products, block_parts(): lax.dot_general(grad_all, book_block, dims_nt, preferred_element_type=jnp...  21.3 us
    convert_element_type x1, other arithmetic, per_device(): delta = delta.astype(jnp.bfloat16)  13.5 us
  transfers between devices with their start and end apart: 2, of which 2 were waited for; matrix products, arithmetic and copies ran while one was open for 4% of the time, Pallas kernels for 0%

commit v1 on v0

--- a/solution.py
+++ b/solution.py
@@ -8,7 +8,9 @@
 
 def per_device(latents, out_grad, targets, codebook):
     lat_all, grad_all = (
-        lax.all_gather(latents, "code", axis=0, tiled=True),
+        jnp.concatenate(
+            lax.all_to_all(jnp.stack([latents] * lax.axis_size("code")), "code", 0, 0), axis=0
+        ),
         lax.all_gather(out_grad, "code", axis=0, tiled=True),
     )
     code_dev, feature_width = codebook.shape

time: 585 us -> 565 us (0.966)
  blocking collectives: 193 us -> 154 us
  starting transfers between devices: 0.08 us -> 12.1 us
    all_gather x1 -> x0, blocking collectives: 41.3 us -> none  [per_device(): lax.all_gather(latents, 'code', axis=0, tiled=True)]
    all_to_all x0 -> x1, starting transfers between devices: none -> 12 us  [per_device(): lax.all_to_all(jnp.stack([latents] * lax.axis_size('code')), 'code', 0, 0)]
  transfers between devices with their start and end apart: 2 -> 3, of which waited for: 2 -> 2; matrix products, arithmetic and copies ran while one was open for 4% -> 6% of each run, Pallas kernels for 0% -> 0%
where the time goes in v1:
time: 565 us; the launch traced here: 564 us
  waiting for transfers between devices  296 us (52%)
  blocking collectives  154 us (27%)
  matrix products  44.5 us (8%)
  other arithmetic  24.2 us (4%)
  local copies, waits for them, and re-layouts  18.8 us (3%)
  between operations  14.3 us (3%)
  starting transfers between devices  12.1 us (2%)
    reduce_scatter x1, waiting for transfers between devices, per_device(): lax.psum_scatter(lat_grad, 'code', scatter_dimension=0, tiled=True)  236 us
    reduce_scatter x1, waiting for transfers between devices, per_device(): lax.psum_scatter(whole, 'dp', scatter_dimension=0, tiled=True)  59.9 us
    pmax x1, blocking collectives, per_device(): peak_value = lax.pmax(top, 'code')  58.4 us
    psum x1, blocking collectives, per_device(): lax.psum((total * rescale, weighted * rescale, picked), 'code')  56.7 us
    all_gather x1, blocking collectives, per_device(): lax.all_gather(out_grad, 'code', axis=0, tiled=True)  39.1 us
    dot_general x4, matrix products, block_parts(): lax.dot_general(grad_all, book_block, dims_nt, preferred_element_type=jnp...  21.2 us
    convert_element_type x1, other arithmetic, per_device(): delta = delta.astype(jnp.bfloat16)  13.5 us
    all_to_all x1, starting transfers between devices, per_device(): lax.all_to_all(jnp.stack([latents] * lax.axis_size('code')), 'code', 0, 0)  12 us
  transfers between devices with their start and end apart: 3, of which 2 were waited for; matrix products, arithmetic and copies ran while one was open for 6% of the time, Pallas kernels for 0%

profile of v1, /device:TPU:1, one launch (start us, length us, event | category | flops | bytes accessed | tf_op | source)
XLA Modules:
  0.0 564.1 jit_solution(1819957416965113240)
XLA Ops:
  7.2 1.4 stack.2
  8.6 12.0 %all-to-all-start = ((bf16[32,16,256]{2,1,0:T(8,128)(2,1)}), bf16[32,16,256]{2,1,0:T(8,128)(2,1)S(1)}, u32[]{:S(2)}, u32[]{:S(2)}) async-start(bf16[32,16,256]{2,1,0:T(8,128)(2,1)} %stack.2), calls=%async_computation | async-start | bytes 524288 | tf_op jit(solution)/shard_map/all_to_all | solution.py:12
  21.0 39.1 %all_gather.3 = bf16[512,256]{1,0:T(8,128)(2,1)S(1)} all-gather(bf16[16,256]{1,0:T(8,128)(2,1)} %param.5), channel_id=1, replica_groups=mesh['dp'=8,'code'=32] {'code'}, dimensions={0}, use_global_device_ids=true | all-gather | bytes 270336 | tf_op jit(solution)/shard_map/all_gather | solution.py:14
  60.1 3.6 fusion.26
  63.7 2.7 fusion.33
  66.4 2.7 fusion.31
  69.1 2.7 fusion.32
  71.8 8.2 %scatter_custom_fusion = f32[8193,256]{1,0:T(8,128)} fusion(s32[512]{0:T(512)S(1)} %get-tuple-element.20, f32[]{:T(128)} %constant.11.clone.1, bf16[512,256]{1,0:T(8,128)(2,1)} %copy-done.11), kind=kCustom, calls=%fused_computation.10 | custom fusion | flops 262144 | bytes 8651780 | tf_op jit(solution)/shard_map/scatter-add | solution.py:66
  80.0 3.4 slice-done
  83.4 3.3 fusion.25
  86.7 2.7 fusion.28
  89.4 2.7 fusion.30
  92.1 2.7 fusion.29
  94.8 2.7 fusion.27
  97.6 58.4 %pmax.7 = f32[512]{0:T(512)S(1)} all-reduce(f32[512]{0:T(512)S(1)} %get-tuple-element.22), channel_id=1, replica_groups=mesh['dp'=8,'code'=32] {'code'}, use_global_device_ids=true, to_apply=%region_4.5 | all-reduce | flops 512 | bytes 4096 | tf_op jit(solution)/shard_map/pmax | solution.py:55
  156.0 13.1 %fusion.18 = (f32[512]{0:T(512)S(1)}, f32[512]{0:T(512)S(1)}, f32[512]{0:T(512)S(1)}, f32[512]{0:T(512)S(1)}, f32[512]{0:T(512)S(1)}, /*index=5*/f32[512]{0:T(51...) fusion(f32[512,2048]{1,0:T(8,128)} %get-tuple-element.50, ...), kind=kOutput, calls=%fused_computation.36 | convolution fusion | flops 566224896 | bytes 34932736 | tf_op jit(solution)/shard_map/dot_general | solution.py:36
  169.2 56.7 %all-reduce = (f32[512]{0:T(512)S(1)}, f32[512]{0:T(512)S(1)}, f32[512]{0:T(512)S(1)}) all-reduce(f32[512]{0:T(512)S(1)} %get-tuple-element.34, f32[512]{0:T(512)S(1)} %get-tuple-element.33, f32[512]{0:T(512)S(1)} %add_add_fusion), channel_id=1, replica_groups=mesh['dp'=8,'code'=32] {'code'}, use_global_device_ids=true, to_apply=%region_14.15 | all-reduce | flops 1536 | bytes 12288 | tf_op jit(solution)/shard_map/psum | solution.py:57
  225.9 13.5 %fusion.16 = (bf16[512,2048]{1,0:T(8,128)(2,1)S(1)}, bf16[512,2048]{1,0:T(8,128)(2,1)S(1)}, bf16[512,2048]{1,0:T(8,128)(2,1)S(1)}, bf16[512,2048]{1,0:T(8,128)(2,1)S(1)}) fusion(f32[512,2048]{1,0:T(8,128)} %fusion.33, f32[512,2048]{1,0:T(8,128)} %get-tuple-element.52, s32[2048]{0:T(1024)S(1)} %bitcast.94, f32[512]{0:T(512)S(1)} %get-tuple-element.39, ...), kind=kLoop, calls=%fused_computation.26 | loop fusion | flops 33554432 | bytes 41981952 | tf_op jit(solution)/shard_map/convert_element_type | solution.py:78
  239.5 2.8 fusion.34
  242.3 1.9 convolution_add_fusion.6
  245.0 1.6 convolution_add_fusion.4
  246.7 3.1 convolution_add_fusion.2
  250.2 0.8 convolution_add_fusion.1
  250.9 0.8 copy-done.1
  252.4 0.7 convolution_add_fusion.3
  253.1 0.8 copy-done.5
  254.0 0.8 convolution_add_fusion
  254.7 0.8 pad_maximum_fusion
  255.6 3.8 copy.8
  260.0 236.1 %reduce-scatter.3.cloned.1.call-done = f32[16,256]{1,0:T(8,128)} async-done(((f32[512,256]{1,0:T(8,128)}), f32[16,256]{1,0:T(8,128)}) %reduce-scatter.3.cloned.1.call-update) | async-done | bytes 16400 | tf_op jit(solution)/shard_map/reduce_scatter | solution.py:87
  496.1 1.3 convert_element_type.38
  497.4 59.9 %reduce-scatter.5.cloned.1.call-done = f32[1024,256]{1,0:T(8,128)} async-done(((f32[8192,256]{1,0:T(8,128)}), f32[1024,256]{1,0:T(8,128)}) %reduce-scatter.5.cloned.1.call-update) | async-done | bytes 1048592 | tf_op jit(solution)/shard_map/reduce_scatter | solution.py:86
  (55 shorter events, 2.8 us)
Async XLA Ops:
  8.6 78.1 %all-to-all-start = ((bf16[32,16,256]{2,1,0:T(8,128)(2,1)}), bf16[32,16,256]{2,1,0:T(8,128)(2,1)S(1)}, u32[]{:S(2)}, u32[]{:S(2)}) async-start(bf16[32,16,256]{2,1,0:T(8,128)(2,1)} %stack.2), calls=%async_computation | async-start | bytes 524288 | tf_op jit(solution)/shard_map/all_to_all | solution.py:12
  20.6 475.4 %reduce-scatter.3.cloned.1.call-start = ((), (), s32[]{:S(2)}) async-start(), calls=%async_computation.3 | async-start | bytes 540672 | tf_op jit(solution)/shard_map/reduce_scatter | solution.py:87
  60.1 9.0 %copy-start.11 = (bf16[512,256]{1,0:T(8,128)(2,1)}, bf16[512,256]{1,0:T(8,128)(2,1)S(1)}, u32[]{:S(2)}) copy-start(bf16[512,256]{1,0:T(8,128)(2,1)S(1)} %all_gather.3) | copy-start | bytes 786436
  63.7 25.7 %copy-start.10 = (bf16[8,1,256,256]{3,2,1,0:T(8,128)(2,1)}, bf16[8,1,256,256]{3,2,1,0:T(8,128)(2,1)S(1)}, u32[]{:S(2)}) copy-start(bf16[8,1,256,256]{3,2,1,0:T(8,128)(2,1)S(1)} %get-tuple-element.29) | copy-start | bytes 3145732
  63.7 28.5 %copy-start.8 = (bf16[8,1,256,256]{3,2,1,0:T(8,128)(2,1)}, bf16[8,1,256,256]{3,2,1,0:T(8,128)(2,1)S(1)}, u32[]{:S(2)}) copy-start(bf16[8,1,256,256]{3,2,1,0:T(8,128)(2,1)S(1)} %get-tuple-element.31) | copy-start | bytes 3145732
  66.4 5.4 copy-start.15
  80.0 3.4 slice-start
  89.4 5.4 copy-start.13
  92.1 63.8 %copy-start.12 = (bf16[512,256]{1,0:T(8,128)(2,1)S(1)}, bf16[512,256]{1,0:T(8,128)(2,1)}, u32[]{:S(2)}) copy-start(bf16[512,256]{1,0:T(8,128)(2,1)} %copy-done.11) | copy-start | bytes 786436
  94.8 61.1 %copy-start.14 = (bf16[8,1,256,256]{3,2,1,0:T(8,128)(2,1)S(1)}, bf16[8,1,256,256]{3,2,1,0:T(8,128)(2,1)}, u32[]{:S(2)}) copy-start(bf16[8,1,256,256]{3,2,1,0:T(8,128)(2,1)} %get-tuple-element.32) | copy-start | bytes 3145732
  239.4 4.8 copy-start
  239.4 4.8 copy-start.4
  239.4 4.8 copy-start.2
  239.5 4.8 copy-start.9
  246.6 310.7 %reduce-scatter.5.cloned.1.call-start = ((), (), s32[]{:S(2)}) async-start(), calls=%async_computation.4 | async-start | bytes 9437184 | tf_op jit(solution)/shard_map/reduce_scatter | solution.py:86
  246.7 3.1 copy-start.3
  246.7 3.5 copy-start.7
  250.1 1.6 copy-start.1
  250.1 2.2 copy-start.6
  252.4 1.6 copy-start.5
Sparse Core Ops, SparseCore 0:
  246.7 249.2 reduce-scatter.2
  499.2 58.0 reduce-scatter.4
